TPU v7x, 512 devices: a whole 4x8x8 slice. The times are simulated.
512 devices in a mesh: cells: 128 (over y, z, core), samp: 4 (over x).
Axes of the slice: x: 4, y: 8, z: 8, core: 2. Of those that a mesh axis runs over, the one named last changes fastest.
Arguments:
- snapshots: bfloat16 [262144, 4096], P('cells', 'samp'), may hold values from -24 to 24
- left_slow: bfloat16 [120, 4096], P(None, 'cells'), may hold values from -0.09375 to 0.09375
- left_fast: bfloat16 [120, 64], replicated, may hold values from -0.75 to 0.75
- right_slow: bfloat16 [150, 128], P(None, 'samp'), may hold values from -0.5 to 0.5
- right_fast: bfloat16 [150, 32], replicated, may hold values from -1 to 1
Outputs:
- range_sketch: float32 [262144, 150], P(('cells', 'samp'))
- core: float32 [150, 4096], P(None, ('samp', 'cells'))
All inputs are finite; a program needn't handle non-finite values.
Results may differ from a plain program's by a relative error of at most 0.012.
The roundings to bfloat16 on the way count: a program that leaves them out, or rounds other values in their place, can miss the bound.
Values sent between devices are 32-bit elements; how exact they have to be, the bound alone decides.
A program may use at most 64 MiB of HBM per device.

v0:
```python
import jax
import jax.numpy as jnp
from jax import lax
from jax.sharding import PartitionSpec as P


def expand(slow, fast):
    rows = slow.shape[0]
    return (
        (slow.astype(jnp.float32)[:, :, None] * fast.astype(jnp.float32)[:, None, :])
        .reshape(rows, -1)
        .astype(jnp.bfloat16)
    )


def on_device(snapshots, left_slow, left_fast, right_slow, right_fast):
    psi = expand(left_slow, left_fast)
    omega = expand(right_slow, right_fast)
    left_term = jnp.dot(psi, snapshots, preferred_element_type=jnp.float32)
    range_term = lax.dot_general(
        snapshots, omega, (((1,), (1,)), ((), ())), preferred_element_type=jnp.float32
    )
    range_part = lax.psum_scatter(range_term, "samp", scatter_dimension=0, tiled=True)
    width = snapshots.shape[1] // lax.axis_size("cells")
    col_start = lax.axis_index("cells") * width
    left_full = lax.psum(left_term, "cells")
    left_part = lax.dynamic_slice_in_dim(left_full, col_start, width, 1)
    height = range_part.shape[0]
    psi_rows = lax.dynamic_slice_in_dim(psi, lax.axis_index("samp") * height, height, 1).astype(
        jnp.float32
    )
    partial_value = jnp.dot(psi_rows, range_part, precision=lax.Precision.HIGHEST)
    core_input = lax.psum(partial_value, ("cells", "samp"))
    rank_left = core_input.shape[0]
    gram = jnp.dot(core_input, core_input.T, precision=lax.Precision.HIGHEST) + 0.5 * jnp.eye(
        rank_left, dtype=jnp.float32
    )
    factor = jnp.linalg.cholesky(gram)
    solved = jax.scipy.linalg.cho_solve((factor, True), left_part)
    core = jnp.dot(core_input.T, solved, precision=lax.Precision.HIGHEST)
    return (range_part, core)


def solution(mesh):
    placed = (P("cells", "samp"), P(None, "cells"), P(), P(None, "samp"), P())
    return jax.shard_map(
        on_device,
        mesh=mesh,
        in_specs=placed,
        out_specs=(P(("cells", "samp"), None), P(None, ("samp", "cells"))),
        check_vma=False,
    )
```

profile of v0, /device:TPU:24, one launch (start us, length us, event | category | flops | bytes accessed | tf_op | source)
XLA Modules:
  0.0 517.7 jit_solution(6661757169224194869)
XLA Ops:
  7.2 0.0 copy-start
  7.2 0.0 copy-start.1
  7.2 0.0 reduce-scatter.2.cloned.1.call-start
  7.2 0.7 convert_element_type.27
  8.0 0.7 convert_element_type.26
  8.7 0.1 multiply_convert_fusion.1
  8.8 4.8 convolution_bitcast_fusion
  13.6 0.0 reduce-scatter.2.cloned.1.call-update
  13.6 0.0 all-reduce.3.cloned.1.call-start
  13.7 0.0 copy-done
  13.7 0.0 copy-done.1
  13.7 0.1 multiply_convert_fusion
  13.9 34.2 %reduce-scatter.2.cloned.1.call-done = f32[512,150]{0,1:T(8,128)} async-done(((f32[2048,150]{0,1:T(8,128)}), f32[512,150]{0,1:T(8,128)}) %reduce-scatter.2.cloned.1.call-update) | async-done | bytes 307216 | tf_op jit(solution)/shard_map/reduce_scatter | solution.py:23
  48.0 1.9 fusion
  49.9 0.0 all-reduce.3.cloned.1.call-update
  49.9 0.0 all-reduce.5.cloned.1.call-start
  50.0 3.7 fusion.13
  53.7 0.0 all-reduce.5.cloned.1.call-update
  53.7 261.5 %all-reduce.3.cloned.1.call-done = f32[120,150]{0,1:T(8,128)} async-done(((f32[120,150]{0,1:T(8,128)}), f32[120,150]{0,1:T(8,128)}) %all-reduce.3.cloned.1.call-update) | async-done | bytes 72016 | tf_op jit(solution)/shard_map/psum | solution.py:33
  315.2 1.4 fusion.12
  316.6 0.1 copy.12
  316.7 11.0 %cholesky.16 = f32[120,120]{1,0:T(8,128)S(1)} custom-call(f32[120,120]{1,0:T(8,128)S(1)} %fusion.8), custom_call_target="Cholesky" | custom-call | tf_op jit(solution)/shard_map/jit(cholesky)/cholesky | solution.py:38
  327.8 0.6 compare_reduce_fusion
  328.4 0.7 fusion.2
  329.1 9.2 %custom-call.10 = f32[1,120,120]{1,2,0:T(8,128)S(1)} custom-call(f32[1,120,120]{2,1,0:T(8,128)S(1)} %fusion.2), custom_call_target="InvertDiagBlocksLowerTriangular" | custom-call | tf_op jit(solution)/shard_map/jit(_cho_solve)/triangular_solve | solution.py:39
  338.3 169.8 %all-reduce.5.cloned.1.call-done = f32[120,1024]{1,0:T(8,128)} async-done(((f32[120,1024]{1,0:T(8,128)}), f32[120,1024]{1,0:T(8,128)}) %all-reduce.5.cloned.1.call-update) | async-done | bytes 491536 | tf_op jit(solution)/shard_map/psum | solution.py:26
  508.0 1.2 fusion.5
  509.2 0.2 fusion.3
  509.5 1.8 fusion.14
  (4 shorter events, 0.1 us)
Async XLA Ops:
  7.2 6.5 %copy-start = (bf16[120,64]{0,1:T(8,128)(2,1)S(1)}, bf16[120,64]{0,1:T(8,128)(2,1)}, u32[]{:S(2)}) copy-start(bf16[120,64]{0,1:T(8,128)(2,1)} %param.7) | copy-start | bytes 46084
  7.2 6.5 %copy-start.1 = (bf16[120,32]{0,1:T(8,128)(2,1)S(1)}, bf16[120,32]{0,1:T(8,128)(2,1)}, u32[]{:S(2)}) copy-start(bf16[120,32]{0,1:T(8,128)(2,1)} %param.6) | copy-start | bytes 23044
  7.2 40.8 %reduce-scatter.2.cloned.1.call-start = ((), (), s32[]{:S(2)}) async-start(), calls=%async_computation.1 | async-start | bytes 1556480 | tf_op jit(solution)/shard_map/reduce_scatter | solution.py:23
  13.6 301.6 %all-reduce.3.cloned.1.call-start = ((), (), s32[]{:S(2)}) async-start(), calls=%async_computation.2 | async-start | bytes 155648 | tf_op jit(solution)/shard_map/psum | solution.py:33
  49.9 458.1 %all-reduce.5.cloned.1.call-start = ((), (), s32[]{:S(2)}) async-start(), calls=%async_computation.3 | async-start | bytes 983040 | tf_op jit(solution)/shard_map/psum | solution.py:26
Sparse Core Ops, SparseCore 0:
  13.7 34.2 reduce-scatter.1
  53.0 262.1 all-reduce.2
  318.5 189.4 all-reduce.4
where the time goes:
time: 518 us
  waiting for transfers between devices  465 us (90%)
  other arithmetic  23.2 us (4%)
  matrix products  15 us (3%)
  between operations  13.9 us (3%)
    psum x1, waiting for transfers between devices, on_device(): core_input = lax.psum(partial_value, ('cells', 'samp'))  261 us
    psum x1, waiting for transfers between devices, on_device(): left_full = lax.psum(left_term, 'cells')  170 us
    reduce_scatter x1, waiting for transfers between devices, on_device(): lax.psum_scatter(range_term, 'samp', scatter_dimension=0, tiled=True)  34.2 us
    another operation x3, other arithmetic, on_device(): factor = jnp.linalg.cholesky(gram)  11.6 us
  transfers between devices with their start and end apart: 3, of which 3 were waited for; matrix products, arithmetic and copies ran while one was open for 5% of the time, Pallas kernels for 0%

commit v1 on v0

--- a/solution.py
+++ b/solution.py
@@ -30,7 +30,9 @@
         jnp.float32
     )
     partial_value = jnp.dot(psi_rows, range_part, precision=lax.Precision.HIGHEST)
-    core_input = lax.psum(partial_value, ("cells", "samp"))
+    core_input = partial_value
+    for over in ("samp", "cells"):
+        core_input = lax.psum(core_input, over)
     rank_left = core_input.shape[0]
     gram = jnp.dot(core_input, core_input.T, precision=lax.Precision.HIGHEST) + 0.5 * jnp.eye(
         rank_left, dtype=jnp.float32

time: 518 us -> 335 us (0.65)
  the two profiles are of different devices: /device:TPU:24 before, /device:TPU:1 now
where the time goes in v1:
time: 335 us
  waiting for transfers between devices  282 us (84%)
  other arithmetic  23.2 us (7%)
  matrix products  14.9 us (4%)
  between operations  13.9 us (4%)
    psum x2, waiting for transfers between devices, on_device(): core_input = lax.psum(core_input, over)  249 us
    reduce_scatter x1, waiting for transfers between devices, on_device(): lax.psum_scatter(range_term, 'samp', scatter_dimension=0, tiled=True)  33.1 us
    another operation x3, other arithmetic, on_device(): factor = jnp.linalg.cholesky(gram)  11.6 us
    another operation x2, other arithmetic, on_device(): solved = jax.scipy.linalg.cho_solve((factor, True), left_part)  9.85 us
  transfers between devices with their start and end apart: 3, of which 3 were waited for; matrix products, arithmetic and copies ran while one was open for 1% of the time, Pallas kernels for 0%

profile of v1, /device:TPU:1, one launch (start us, length us, event | category | flops | bytes accessed | tf_op | source)
XLA Modules:
  0.0 334.7 jit_solution(13868642109355701146)
XLA Ops:
  7.2 0.0 copy-start
  7.2 0.0 copy-start.1
  7.2 0.0 reduce-scatter.2.cloned.1.call-start
  7.2 0.7 convert_element_type.27
  8.0 0.7 convert_element_type.26
  8.7 0.1 multiply_convert_fusion.1
  8.8 4.8 %convolution_bitcast_fusion = f32[2048,150]{0,1:T(8,128)} fusion(bf16[150,1024]{0,1:T(8,128)(2,1)S(1)} %bitcast.29, bf16[2048,1024]{1,0:T(8,128)(2,1)} %param.5), kind=kOutput, calls=%fused_computation | convolution fusion | flops 629145600 | bytes 5730304 | tf_op jit(solution)/shard_map/dot_general | solution.py:20
  13.6 0.0 reduce-scatter.2.cloned.1.call-update
  13.6 0.0 all-reduce.4.cloned.1.call-start
  13.7 0.0 copy-done
  13.7 0.0 copy-done.1
  13.7 0.1 multiply_convert_fusion
  13.9 33.1 %reduce-scatter.2.cloned.1.call-done = f32[512,150]{0,1:T(8,128)} async-done(((f32[2048,150]{0,1:T(8,128)}), f32[512,150]{0,1:T(8,128)}) %reduce-scatter.2.cloned.1.call-update) | async-done | bytes 307216 | tf_op jit(solution)/shard_map/reduce_scatter | solution.py:23
  46.9 1.9 fusion
  48.8 0.0 all-reduce.4.cloned.1.call-update
  48.8 0.0 all-reduce.6.cloned.1.call-start
  48.9 3.7 %fusion.13 = f32[120,1024]{1,0:T(8,128)} fusion(bf16[120,2048]{0,1:T(8,128)(2,1)S(1)} %bitcast.28, bf16[2048,1024]{1,0:T(8,128)(2,1)} %param.5), kind=kOutput, calls=%fused_computation.23 | convolution fusion | flops 503316480 | bytes 5177344 | tf_op jit(solution)/shard_map/dot_general | solution.py:19
  52.6 47.6 %all-reduce.4.cloned.1.call-done = f32[120,150]{0,1:T(8,128)} async-done(((f32[120,150]{0,1:T(8,128)}), f32[120,150]{0,1:T(8,128)}) %all-reduce.4.cloned.1.call-update) | async-done | bytes 72016 | tf_op jit(solution)/shard_map/psum | solution.py:35
  100.2 0.0 all-reduce.6.cloned.1.call-update
  100.2 201.8 %all-reduce.6.cloned.1.call-done = (f32[120,150]{0,1:T(8,128)}, f32[120,1024]{1,0:T(8,128)}) async-done(((f32[120,150]{0,1:T(8,128)}, f32[120,1024]{1,0:T(8,128)}), (f32[120,150]{0,1:T(8,128)}, f32[120,1024]{1,0:T(8,128)})) %all-reduce.6.cloned.1.call-update) | async-done | bytes 563536 | tf_op jit(solution)/shard_map/psum | solution.py:35
  301.9 1.4 fusion.12
  303.3 0.1 copy.12
  303.5 11.0 %cholesky.16 = f32[120,120]{1,0:T(8,128)S(1)} custom-call(f32[120,120]{1,0:T(8,128)S(1)} %fusion.8), custom_call_target="Cholesky" | custom-call | tf_op jit(solution)/shard_map/jit(cholesky)/cholesky | solution.py:40
  314.5 0.6 compare_reduce_fusion
  315.1 0.7 fusion.2
  315.8 9.2 %custom-call.10 = f32[1,120,120]{1,2,0:T(8,128)S(1)} custom-call(f32[1,120,120]{2,1,0:T(8,128)S(1)} %fusion.2), custom_call_target="InvertDiagBlocksLowerTriangular" | custom-call | tf_op jit(solution)/shard_map/jit(_cho_solve)/triangular_solve | solution.py:41
  325.0 1.2 fusion.5
  326.2 0.3 fusion.3
  326.4 1.8 fusion.14
  (4 shorter events, 0.1 us)
Async XLA Ops:
  7.2 6.5 %copy-start = (bf16[120,64]{0,1:T(8,128)(2,1)S(1)}, bf16[120,64]{0,1:T(8,128)(2,1)}, u32[]{:S(2)}) copy-start(bf16[120,64]{0,1:T(8,128)(2,1)} %param.7) | copy-start | bytes 46084
  7.2 6.5 %copy-start.1 = (bf16[120,32]{0,1:T(8,128)(2,1)S(1)}, bf16[120,32]{0,1:T(8,128)(2,1)}, u32[]{:S(2)}) copy-start(bf16[120,32]{0,1:T(8,128)(2,1)} %param.6) | copy-start | bytes 23044
  7.2 39.8 %reduce-scatter.2.cloned.1.call-start = ((), (), s32[]{:S(2)}) async-start(), calls=%async_computation.1 | async-start | bytes 1556480 | tf_op jit(solution)/shard_map/reduce_scatter | solution.py:23
  13.6 86.5 %all-reduce.4.cloned.1.call-start = ((), (), s32[]{:S(2)}) async-start(), calls=%async_computation.2 | async-start | bytes 155648 | tf_op jit(solution)/shard_map/psum | solution.py:35
  48.8 253.1 %all-reduce.6.cloned.1.call-start = ((), (), s32[]{:S(2)}) async-start(), calls=%async_computation.3 | async-start | bytes 1138688 | tf_op jit(solution)/shard_map/psum | solution.py:35
Sparse Core Ops, SparseCore 0:
  13.7 33.1 reduce-scatter.1
  49.3 50.8 all-reduce.3
  103.6 198.3 all-reduce.5
